TPU v7x, 128 devices: a whole 4x4x4 slice. The times are simulated.
128 devices in a mesh: wide: 8 (over z_hi, y), narrow: 16 (over z_lo, x, core).
Axes of the slice: x: 4, y: 4, z: 4 (z_hi: 2, z_lo: 2; z = z_hi * 2 + z_lo), core: 2. Of those that a mesh axis runs over, the one named last changes fastest.
Arguments:
- features: bfloat16 [262144, 128], P(('wide', 'narrow')), may hold values from -6 to 6
- band_tiles: int32 [2048, 16, 128, 128], P(('wide', 'narrow')), may hold values 0 or 1
- band_cols: int32 [2048, 16], P(('wide', 'narrow')), may hold values from 0 to 15
- off_tiles: int32 [128, 8, 128, 128], P(('wide', 'narrow')), may hold values 0 or 1
- req_block: int32 [128, 8], P(('wide', 'narrow')), may hold values from 0 to 15
- req_row: int32 [128, 8], P(('wide', 'narrow')), may hold values from 0 to 15
- req_valid: int32 [128, 8], P(('wide', 'narrow')), may hold values 0 or 1
- weight_self: bfloat16 [128, 256], replicated, may hold values from -0.5 to 0.5
- weight_neigh: bfloat16 [128, 256], replicated, may hold values from -1.5 to 1.5
- bias_term: bfloat16 [256], replicated, may hold values from -3 to 3
- cotangent: bfloat16 [262144, 256], P(('wide', 'narrow')), may hold values from -6 to 6
Outputs:
- layer_out: bfloat16 [262144, 256], P(('wide', 'narrow'))
- grad_features: float32 [262144, 128], P(('wide', 'narrow'))
- grad_self: float32 [128, 256], replicated
- grad_neigh: float32 [128, 256], replicated
- grad_bias: float32 [256], replicated
All inputs are finite; a program needn't handle non-finite values. No bound on the sum of `band_tiles` or of `off_tiles` or of `req_valid` on one device may be relied on, other than what follows from the above.
Results may differ from a plain program's by a relative error of at most 0.007.
Values may be sent and summed in bfloat16 or wider, within the bound.
A program may use at most 128 MiB of HBM per device.

v0:
```python
from functools import partial

import jax
import jax.numpy as jnp
from jax import lax
from jax.sharding import PartitionSpec as P


def passed_along(x, axis, by):
    peers = lax.axis_size(axis)
    return lax.ppermute(x, axis, [(i, (i + by) % peers) for i in range(peers)])


def shards(
    features,
    band_tiles,
    band_cols,
    off_tiles,
    req_block,
    req_row,
    req_valid,
    weight_self,
    weight_neigh,
    bias_term,
    cotangent,
):
    row_count, in_width = features.shape
    block_count = band_tiles.shape[0]
    block_size = band_tiles.shape[2]
    loop_size = lax.axis_size("narrow")
    wide_size = lax.axis_size("wide")
    my_index = lax.axis_index("narrow")
    highest = lax.Precision.HIGHEST
    tile_half = band_tiles.astype(jnp.bfloat16)
    block_ids = jnp.arange(block_count, dtype=jnp.int32)

    def band_add(totals, current, which):
        columns = lax.dynamic_index_in_dim(band_cols, which, 1, keepdims=False)
        tiles_now = lax.dynamic_index_in_dim(tile_half, which, 1, keepdims=False)
        picked = jnp.take(current.reshape(block_count, block_size, in_width), columns, axis=0)
        return totals + jnp.einsum(
            "bij,bjf->bif", tiles_now, picked, preferred_element_type=jnp.float32
        )

    start_totals = band_add(
        jnp.zeros((block_count, block_size, in_width), jnp.float32), features, my_index
    )

    def advance_one(offset, state_in):
        current, totals = state_in
        current = passed_along(current, "narrow", 1)
        return (current, band_add(totals, current, (my_index - offset) % loop_size))

    _, band_sum = lax.fori_loop(1, loop_size, advance_one, (features, start_totals))
    ask_ids = req_block[0]
    row_slots = req_row[0]
    off_mask = (off_tiles[0] * req_valid[0][:, None, None]).astype(jnp.bfloat16)
    placing = (row_slots[:, None] == block_ids[None, :]).astype(jnp.float32)
    whole_group = lax.all_gather(features, "wide", axis=0, tiled=True).reshape(
        wide_size, block_count, block_size, in_width
    )
    fetched = whole_group[jnp.arange(wide_size), ask_ids]
    pulled = jnp.einsum("wij,wjf->wif", off_mask, fetched, preferred_element_type=jnp.float32)
    gathered = band_sum + jnp.einsum("wb,wif->bif", placing, pulled, precision=highest)
    off_degree = jnp.sum(off_mask.astype(jnp.float32), axis=2)
    degree = jnp.sum(band_tiles.astype(jnp.float32), axis=(1, 3)) + jnp.einsum(
        "wb,wi->bi", placing, off_degree, precision=highest
    )
    denom = degree + 1.0
    aggregate = (gathered / denom[:, :, None]).reshape(row_count, in_width).astype(jnp.bfloat16)
    pre = jnp.dot(features, weight_self, preferred_element_type=jnp.float32)
    pre = (
        pre
        + jnp.dot(aggregate, weight_neigh, preferred_element_type=jnp.float32)
        + bias_term.astype(jnp.float32)
    )
    activated, pullback = jax.vjp(partial(jax.nn.gelu, approximate=True), pre)
    layer_out = activated.astype(jnp.bfloat16)
    grad_pre = pullback(cotangent.astype(jnp.float32))[0].astype(jnp.bfloat16)
    local_self = jnp.dot(features.T, grad_pre, preferred_element_type=jnp.float32)
    local_neigh = jnp.dot(aggregate.T, grad_pre, preferred_element_type=jnp.float32)
    local_bias = jnp.sum(grad_pre.astype(jnp.float32), axis=0)
    total_self, total_neigh, total_bias = lax.psum(
        (local_self, local_neigh, local_bias), ("wide", "narrow")
    )
    factor = (wide_size * loop_size * row_count) ** (-0.5)
    grad_agg = jnp.dot(grad_pre, weight_neigh.T, preferred_element_type=jnp.float32)
    signal = (grad_agg.reshape(block_count, block_size, in_width) / denom[:, :, None]).astype(
        jnp.bfloat16
    )
    slab_count = row_count * lax.axis_size("narrow") // row_count
    moved = jnp.einsum("bsji,bjf->sbif", tile_half, signal, preferred_element_type=jnp.float32)
    one_hot = (band_cols.T[:, :, None] == block_ids[None, None, :]).astype(jnp.float32)
    placed = jnp.einsum("sbt,sbif->stif", one_hot, moved, precision=highest)
    band_back = lax.psum_scatter(
        placed.reshape(slab_count * row_count, in_width).astype(jnp.bfloat16),
        "narrow",
        scatter_dimension=0,
        tiled=True,
    ).astype(jnp.float32)
    signal_rows = jnp.take(signal, row_slots, axis=0)
    pushed = jnp.einsum("wji,wjf->wif", off_mask, signal_rows, preferred_element_type=jnp.float32)
    peer_count = row_count * lax.axis_size("wide") // row_count
    owner_hot = (ask_ids[:, None] == block_ids[None, :]).astype(jnp.float32)
    placed = jnp.einsum("sb,sif->sbif", owner_hot, pushed, precision=highest)
    off_back = lax.psum_scatter(
        placed.reshape(peer_count * row_count, in_width).astype(jnp.bfloat16),
        "wide",
        scatter_dimension=0,
        tiled=True,
    ).astype(jnp.float32)
    grad_features = jnp.dot(grad_pre, weight_self.T, preferred_element_type=jnp.float32) + (
        band_back + off_back
    )
    return (
        layer_out,
        grad_features,
        total_self * factor,
        total_neigh * factor,
        total_bias * factor,
    )


def solution(mesh):
    placed = (
        P(("wide", "narrow"), None),
        P(("wide", "narrow"), None, None, None),
        P(("wide", "narrow"), None),
        P(("wide", "narrow"), None, None, None),
        P(("wide", "narrow"), None),
        P(("wide", "narrow"), None),
        P(("wide", "narrow"), None),
        P(),
        P(),
        P(),
        P(("wide", "narrow"), None),
    )
    return jax.shard_map(
        shards,
        mesh=mesh,
        in_specs=placed,
        out_specs=(P(("wide", "narrow"), None), P(("wide", "narrow"), None), P(), P(), P()),
        check_vma=False,
    )
```

profile of v0, /device:TPU:1, one launch (start us, length us, event | category | flops | bytes accessed | tf_op | source)
XLA Modules:
  0.0 598.2 jit_solution(16910321590189033704)
XLA Ops:
  8.0 1.0 copy.61
  9.0 1.2 convert_element_type.63
  10.2 1.4 copy.28
  11.6 1.3 convert_reduce_fusion.2
  13.0 7.0 %convert_reduce_fusion = f32[16,128]{1,0:T(8,128)S(1)} fusion(s32[16,16,128,128]{3,2,1,0:T(8,128)} %param.16), kind=kLoop, calls=%fused_computation.18 | loop fusion | flops 8386560 | bytes 16785408 | tf_op jit(solution)/shard_map/reduce_sum | solution.py:66
  23.1 7.3 %copy_convert_fusion = bf16[16,16,128,128]{3,2,0,1:T(8,128)(2,1)S(1)} fusion(s32[16,16,128,128]{3,2,1,0:T(8,128)} %param.16), kind=kLoop, calls=%fused_computation.17 | loop fusion | flops 4194304 | bytes 25165824 | tf_op jit(solution)/shard_map/convert_element_type | solution.py:34
  30.4 3.2 copy-done.2
  34.5 1.7 fusion.60
  36.2 48.6 %all-gather.2.cloned.1.call-done = bf16[16384,128]{1,0:T(8,128)(2,1)} async-done(((bf16[2048,128]{1,0:T(8,128)(2,1)}), bf16[16384,128]{1,0:T(8,128)(2,1)}) %all-gather.2.cloned.1.call-update) | async-done | bytes 4194320 | tf_op jit(solution)/shard_map/all_gather | solution.py:59
  84.8 2.8 gather_fusion.1
  87.8 188.0 %while.17 = (s32[]{:T(128)}, bf16[2048,128]{1,0:T(8,128)(2,1)S(1)}, f32[16,128,128]{2,1,0:T(8,128)S(1)}, s32[]{:T(128)}, bf16[16,16,128,128]{3,2,0,1:T(8,128)(2,...) while((s32[]{:T(128)}, bf16[2048,128]{1,0:T(8,128)(2,1)S(1)}, ...), condition=%wide.region_1.3_spmd, body=%wide.region_0.2_spmd.sunk | while | flops 67634288 | bytes 7344720 | solution.py:54
  87.9 2.2 collective-permute-start
  90.8 5.4 collective-permute-done
  96.9 1.6 convolution_add_fusion.6
  98.5 2.5 collective-permute-start
  101.8 5.4 collective-permute-done
  107.8 1.6 convolution_add_fusion.6
  109.5 2.5 collective-permute-start
  112.7 5.4 collective-permute-done
  118.8 1.6 convolution_add_fusion.6
  120.4 2.5 collective-permute-start
  123.7 6.0 collective-permute-done
  130.3 1.6 convolution_add_fusion.6
  131.9 2.0 collective-permute-start
  134.7 8.1 %collective-permute-done = bf16[2048,128]{1,0:T(8,128)(2,1)S(1)} collective-permute-done((bf16[2048,128]{1,0:T(8,128)(2,1)S(1)}, bf16[2048,128]{1,0:T(8,128)(2,1)S(1)}, u32[]{:S(2)}, u32[]{:S(2)}) %collective-permute-start) | collective-permute-done | bytes 524320 | tf_op jit(solution)/shard_map/while/body/eval_jaxpr/ppermute | solution.py:11
  143.4 1.6 convolution_add_fusion.6
  145.8 10.0 %collective-permute-done = bf16[2048,128]{1,0:T(8,128)(2,1)S(1)} collective-permute-done((bf16[2048,128]{1,0:T(8,128)(2,1)S(1)}, bf16[2048,128]{1,0:T(8,128)(2,1)S(1)}, u32[]{:S(2)}, u32[]{:S(2)}) %collective-permute-start) | collective-permute-done | bytes 524320 | tf_op jit(solution)/shard_map/while/body/eval_jaxpr/ppermute | solution.py:11
  156.5 1.6 convolution_add_fusion.6
  158.9 10.0 %collective-permute-done = bf16[2048,128]{1,0:T(8,128)(2,1)S(1)} collective-permute-done((bf16[2048,128]{1,0:T(8,128)(2,1)S(1)}, bf16[2048,128]{1,0:T(8,128)(2,1)S(1)}, u32[]{:S(2)}, u32[]{:S(2)}) %collective-permute-start) | collective-permute-done | bytes 524320 | tf_op jit(solution)/shard_map/while/body/eval_jaxpr/ppermute | solution.py:11
  169.6 1.6 convolution_add_fusion.6
  172.0 10.0 %collective-permute-done = bf16[2048,128]{1,0:T(8,128)(2,1)S(1)} collective-permute-done((bf16[2048,128]{1,0:T(8,128)(2,1)S(1)}, bf16[2048,128]{1,0:T(8,128)(2,1)S(1)}, u32[]{:S(2)}, u32[]{:S(2)}) %collective-permute-start) | collective-permute-done | bytes 524320 | tf_op jit(solution)/shard_map/while/body/eval_jaxpr/ppermute | solution.py:11
  182.6 1.6 convolution_add_fusion.6
  185.1 10.0 %collective-permute-done = bf16[2048,128]{1,0:T(8,128)(2,1)S(1)} collective-permute-done((bf16[2048,128]{1,0:T(8,128)(2,1)S(1)}, bf16[2048,128]{1,0:T(8,128)(2,1)S(1)}, u32[]{:S(2)}, u32[]{:S(2)}) %collective-permute-start) | collective-permute-done | bytes 524320 | tf_op jit(solution)/shard_map/while/body/eval_jaxpr/ppermute | solution.py:11
  195.7 1.6 convolution_add_fusion.6
  198.2 10.0 %collective-permute-done = bf16[2048,128]{1,0:T(8,128)(2,1)S(1)} collective-permute-done((bf16[2048,128]{1,0:T(8,128)(2,1)S(1)}, bf16[2048,128]{1,0:T(8,128)(2,1)S(1)}, u32[]{:S(2)}, u32[]{:S(2)}) %collective-permute-start) | collective-permute-done | bytes 524320 | tf_op jit(solution)/shard_map/while/body/eval_jaxpr/ppermute | solution.py:11
  208.8 1.6 convolution_add_fusion.6
  211.3 10.0 %collective-permute-done = bf16[2048,128]{1,0:T(8,128)(2,1)S(1)} collective-permute-done((bf16[2048,128]{1,0:T(8,128)(2,1)S(1)}, bf16[2048,128]{1,0:T(8,128)(2,1)S(1)}, u32[]{:S(2)}, u32[]{:S(2)}) %collective-permute-start) | collective-permute-done | bytes 524320 | tf_op jit(solution)/shard_map/while/body/eval_jaxpr/ppermute | solution.py:11
  221.9 1.6 convolution_add_fusion.6
  224.3 10.0 %collective-permute-done = bf16[2048,128]{1,0:T(8,128)(2,1)S(1)} collective-permute-done((bf16[2048,128]{1,0:T(8,128)(2,1)S(1)}, bf16[2048,128]{1,0:T(8,128)(2,1)S(1)}, u32[]{:S(2)}, u32[]{:S(2)}) %collective-permute-start) | collective-permute-done | bytes 524320 | tf_op jit(solution)/shard_map/while/body/eval_jaxpr/ppermute | solution.py:11
  235.0 1.6 convolution_add_fusion.6
  237.4 10.0 %collective-permute-done = bf16[2048,128]{1,0:T(8,128)(2,1)S(1)} collective-permute-done((bf16[2048,128]{1,0:T(8,128)(2,1)S(1)}, bf16[2048,128]{1,0:T(8,128)(2,1)S(1)}, u32[]{:S(2)}, u32[]{:S(2)}) %collective-permute-start) | collective-permute-done | bytes 524320 | tf_op jit(solution)/shard_map/while/body/eval_jaxpr/ppermute | solution.py:11
  248.0 1.6 convolution_add_fusion.6
  250.5 10.0 %collective-permute-done = bf16[2048,128]{1,0:T(8,128)(2,1)S(1)} collective-permute-done((bf16[2048,128]{1,0:T(8,128)(2,1)S(1)}, bf16[2048,128]{1,0:T(8,128)(2,1)S(1)}, u32[]{:S(2)}, u32[]{:S(2)}) %collective-permute-start) | collective-permute-done | bytes 524320 | tf_op jit(solution)/shard_map/while/body/eval_jaxpr/ppermute | solution.py:11
  261.1 1.6 convolution_add_fusion.6
  263.6 10.0 %collective-permute-done = bf16[2048,128]{1,0:T(8,128)(2,1)S(1)} collective-permute-done((bf16[2048,128]{1,0:T(8,128)(2,1)S(1)}, bf16[2048,128]{1,0:T(8,128)(2,1)S(1)}, u32[]{:S(2)}, u32[]{:S(2)}) %collective-permute-start) | collective-permute-done | bytes 524320 | tf_op jit(solution)/shard_map/while/body/eval_jaxpr/ppermute | solution.py:11
  274.2 1.6 convolution_add_fusion.6
  275.9 2.2 fusion.26
  278.3 3.0 convert_reduce_fusion.1
  281.2 1.2 fusion.63
  282.4 1.1 convolution_bitcast_fusion
  284.9 1.4 gather_fusion.2
  286.3 1.2 fusion.38
  287.6 2.9 multiply_convert_fusion
  291.5 11.5 %fusion.9 = f32[16,128,16,128]{3,1,2,0:T(8,128)} fusion(bf16[16,16,128,128]{3,2,0,1:T(8,128)(2,1)} %get-tuple-element.285, bf16[16,128,128,1]{2,0,1,3:T(8,128)(2,1)S(1)} %fusion.80), kind=kOutput, calls=%fused_computation.19 | convolution fusion | flops 1073741824 | bytes 25690112 | tf_op jit(solution)/shard_map/bsji,bjf->sbif/dot_general | solution.py:92
  303.0 17.7 %copy.43 = f32[16,128,16,128]{1,0,3,2:T(8,128)} copy(f32[16,128,16,128]{3,1,2,0:T(8,128)} %fusion.9) | data formatting | bytes 33554432 | tf_op jit(solution)/shard_map/bsji,bjf->sbif/dot_general | solution.py:92
  320.6 14.3 %fusion.11 = bf16[16,16,128,128]{3,1,2,0:T(8,128)(2,1)} fusion(f32[16,128,16,128]{1,0,3,2:T(8,128)} %copy.43, s32[16,16]{1,0:T(8,128)S(1)} %copy.32), kind=kOutput, calls=%fused_computation.22 | convolution fusion | flops 809504768 | bytes 25166848 | tf_op jit(solution)/shard_map/sbt,sbif->stif/dot_general | solution.py:94
  335.0 9.1 %copy.34 = bf16[16,16,128,128]{3,2,1,0:T(8,128)(2,1)} copy(bf16[16,16,128,128]{3,1,2,0:T(8,128)(2,1)} %fusion.11) | data formatting | bytes 16777216 | tf_op jit(solution)/shard_map/convert_element_type | solution.py:96
  344.1 71.1 %psum.23 = f32[256]{0:T(256)S(1)} all-reduce(f32[256]{0:T(256)S(1)} %get-tuple-element.200), channel_id=1, replica_groups=mesh['wide'=8,'narrow'=16] {'wide','narrow'}, use_global_device_ids=true, to_apply=%region_9.11 | all-reduce | flops 256 | bytes 2048 | tf_op jit(solution)/shard_map/psum | solution.py:83
  415.8 15.2 %all-reduce.3.cloned.1.call-done = (f32[128,256]{0,1:T(8,128)}, f32[128,256]{0,1:T(8,128)}) async-done(((f32[128,256]{0,1:T(8,128)}, f32[128,256]{0,1:T(8,128)}), (f32[128,256]{0,1:T(8,128)}, f32[128,256]{0,1:T(8,128)})) %all-reduce.3.cloned.1.call-update) | async-done | bytes 262160 | tf_op jit(solution)/shard_map/psum | solution.py:83
  431.0 1.0 broadcast_multiply_fusion
  432.0 0.8 copy.39
  433.5 82.9 %reduce-scatter.5.cloned.1.call-done = bf16[2048,128]{1,0:T(8,128)(2,1)} async-done(((bf16[16384,128]{1,0:T(8,128)(2,1)}), bf16[2048,128]{1,0:T(8,128)(2,1)}) %reduce-scatter.5.cloned.1.call-update) | async-done | bytes 524304 | tf_op jit(solution)/shard_map/reduce_scatter | solution.py:106
  516.4 72.7 %reduce-scatter.3.cloned.1.call-done = bf16[2048,128]{1,0:T(8,128)(2,1)} async-done(((bf16[32768,128]{1,0:T(8,128)(2,1)}), bf16[2048,128]{1,0:T(8,128)(2,1)}) %reduce-scatter.3.cloned.1.call-update) | async-done | bytes 524304 | tf_op jit(solution)/shard_map/reduce_scatter | solution.py:95
  589.1 2.6 convolution_add_fusion.2
  (127 shorter events, 30.3 us)
Async XLA Ops:
  7.2 271.1 %copy-start = (bf16[128,256]{1,0:T(8,128)(2,1)S(1)}, bf16[128,256]{1,0:T(8,128)(2,1)}, u32[]{:S(2)}) copy-start(bf16[128,256]{1,0:T(8,128)(2,1)} %param.23) | copy-start | bytes 196612
  7.2 77.6 %all-gather.2.cloned.1.call-start = ((), (), s32[]{:S(2)}) async-start(), calls=%async_computation.2 | async-start | bytes 4718592 | tf_op jit(solution)/shard_map/all_gather | solution.py:59
  7.9 423.0 %all-reduce.3.cloned.1.call-start = ((), (), s32[]{:S(2)}) async-start(), calls=%async_computation.5 | async-start | bytes 524288 | tf_op jit(solution)/shard_map/psum | solution.py:83
  12.9 7.0 %copy-start.12 = (s32[1,8]{1,0:T(1,128)S(1)}, s32[1,8]{1,0:T(1,128)}, u32[]{:S(2)}) copy-start(s32[1,8]{1,0:T(1,128)} %param.20) | copy-start | bytes 100
  12.9 7.4 %copy-start.7 = (s32[16,16]{1,0:T(8,128)S(1)}, s32[16,16]{1,0:T(8,128)}, u32[]{:S(2)}) copy-start(s32[16,16]{1,0:T(8,128)} %param.17) | copy-start | bytes 3076
  13.0 7.6 %copy-start.3 = (bf16[2048,128]{1,0:T(8,128)(2,1)S(1)}, bf16[2048,128]{1,0:T(8,128)(2,1)}, u32[]{:S(2)}) copy-start(bf16[2048,128]{1,0:T(8,128)(2,1)} %param.15) | copy-start | bytes 1572868
  13.0 9.5 %copy-start.10 = (s32[1,8]{1,0:T(1,128)S(1)}, s32[1,8]{1,0:T(1,128)}, u32[]{:S(2)}) copy-start(s32[1,8]{1,0:T(1,128)} %param.19) | copy-start | bytes 100
  30.4 3.2 copy-start.2
  33.6 0.8 copy-start.5
  87.9 8.3 %collective-permute-start = (bf16[2048,128]{1,0:T(8,128)(2,1)S(1)}, bf16[2048,128]{1,0:T(8,128)(2,1)S(1)}, u32[]{:S(2)}, u32[]{:S(2)}) collective-permute-start(bf16[2048,128]{1,0:T(8,128)(2,1)S(1)} %get-tuple-element.259), channel_id=1, source_target_pairs={{0,1},{1,2},{2,3},{3,4},{4,5},{5,6},{6,7},{7,8},{8,9},{9,10},{10,1... | collective-permute-start | bytes 1572872 | tf_op jit(solution)/shard_map/while/body/eval_jaxpr/ppermute | solution.py:11
  98.5 8.7 %collective-permute-start = (bf16[2048,128]{1,0:T(8,128)(2,1)S(1)}, bf16[2048,128]{1,0:T(8,128)(2,1)S(1)}, u32[]{:S(2)}, u32[]{:S(2)}) collective-permute-start(bf16[2048,128]{1,0:T(8,128)(2,1)S(1)} %get-tuple-element.259), channel_id=1, source_target_pairs={{0,1},{1,2},{2,3},{3,4},{4,5},{5,6},{6,7},{7,8},{8,9},{9,10},{10,1... | collective-permute-start | bytes 1572872 | tf_op jit(solution)/shard_map/while/body/eval_jaxpr/ppermute | solution.py:11
  109.5 8.7 %collective-permute-start = (bf16[2048,128]{1,0:T(8,128)(2,1)S(1)}, bf16[2048,128]{1,0:T(8,128)(2,1)S(1)}, u32[]{:S(2)}, u32[]{:S(2)}) collective-permute-start(bf16[2048,128]{1,0:T(8,128)(2,1)S(1)} %get-tuple-element.259), channel_id=1, source_target_pairs={{0,1},{1,2},{2,3},{3,4},{4,5},{5,6},{6,7},{7,8},{8,9},{9,10},{10,1... | collective-permute-start | bytes 1572872 | tf_op jit(solution)/shard_map/while/body/eval_jaxpr/ppermute | solution.py:11
  120.4 9.2 %collective-permute-start = (bf16[2048,128]{1,0:T(8,128)(2,1)S(1)}, bf16[2048,128]{1,0:T(8,128)(2,1)S(1)}, u32[]{:S(2)}, u32[]{:S(2)}) collective-permute-start(bf16[2048,128]{1,0:T(8,128)(2,1)S(1)} %get-tuple-element.259), channel_id=1, source_target_pairs={{0,1},{1,2},{2,3},{3,4},{4,5},{5,6},{6,7},{7,8},{8,9},{9,10},{10,1... | collective-permute-start | bytes 1572872 | tf_op jit(solution)/shard_map/while/body/eval_jaxpr/ppermute | solution.py:11
  131.9 10.8 %collective-permute-start = (bf16[2048,128]{1,0:T(8,128)(2,1)S(1)}, bf16[2048,128]{1,0:T(8,128)(2,1)S(1)}, u32[]{:S(2)}, u32[]{:S(2)}) collective-permute-start(bf16[2048,128]{1,0:T(8,128)(2,1)S(1)} %get-tuple-element.259), channel_id=1, source_target_pairs={{0,1},{1,2},{2,3},{3,4},{4,5},{5,6},{6,7},{7,8},{8,9},{9,10},{10,1... | collective-permute-start | bytes 1572872 | tf_op jit(solution)/shard_map/while/body/eval_jaxpr/ppermute | solution.py:11
  145.0 10.8 %collective-permute-start = (bf16[2048,128]{1,0:T(8,128)(2,1)S(1)}, bf16[2048,128]{1,0:T(8,128)(2,1)S(1)}, u32[]{:S(2)}, u32[]{:S(2)}) collective-permute-start(bf16[2048,128]{1,0:T(8,128)(2,1)S(1)} %get-tuple-element.259), channel_id=1, source_target_pairs={{0,1},{1,2},{2,3},{3,4},{4,5},{5,6},{6,7},{7,8},{8,9},{9,10},{10,1... | collective-permute-start | bytes 1572872 | tf_op jit(solution)/shard_map/while/body/eval_jaxpr/ppermute | solution.py:11
  158.1 10.8 %collective-permute-start = (bf16[2048,128]{1,0:T(8,128)(2,1)S(1)}, bf16[2048,128]{1,0:T(8,128)(2,1)S(1)}, u32[]{:S(2)}, u32[]{:S(2)}) collective-permute-start(bf16[2048,128]{1,0:T(8,128)(2,1)S(1)} %get-tuple-element.259), channel_id=1, source_target_pairs={{0,1},{1,2},{2,3},{3,4},{4,5},{5,6},{6,7},{7,8},{8,9},{9,10},{10,1... | collective-permute-start | bytes 1572872 | tf_op jit(solution)/shard_map/while/body/eval_jaxpr/ppermute | solution.py:11
  171.2 10.8 %collective-permute-start = (bf16[2048,128]{1,0:T(8,128)(2,1)S(1)}, bf16[2048,128]{1,0:T(8,128)(2,1)S(1)}, u32[]{:S(2)}, u32[]{:S(2)}) collective-permute-start(bf16[2048,128]{1,0:T(8,128)(2,1)S(1)} %get-tuple-element.259), channel_id=1, source_target_pairs={{0,1},{1,2},{2,3},{3,4},{4,5},{5,6},{6,7},{7,8},{8,9},{9,10},{10,1... | collective-permute-start | bytes 1572872 | tf_op jit(solution)/shard_map/while/body/eval_jaxpr/ppermute | solution.py:11
  184.3 10.8 %collective-permute-start = (bf16[2048,128]{1,0:T(8,128)(2,1)S(1)}, bf16[2048,128]{1,0:T(8,128)(2,1)S(1)}, u32[]{:S(2)}, u32[]{:S(2)}) collective-permute-start(bf16[2048,128]{1,0:T(8,128)(2,1)S(1)} %get-tuple-element.259), channel_id=1, source_target_pairs={{0,1},{1,2},{2,3},{3,4},{4,5},{5,6},{6,7},{7,8},{8,9},{9,10},{10,1... | collective-permute-start | bytes 1572872 | tf_op jit(solution)/shard_map/while/body/eval_jaxpr/ppermute | solution.py:11
  197.4 10.8 %collective-permute-start = (bf16[2048,128]{1,0:T(8,128)(2,1)S(1)}, bf16[2048,128]{1,0:T(8,128)(2,1)S(1)}, u32[]{:S(2)}, u32[]{:S(2)}) collective-permute-start(bf16[2048,128]{1,0:T(8,128)(2,1)S(1)} %get-tuple-element.259), channel_id=1, source_target_pairs={{0,1},{1,2},{2,3},{3,4},{4,5},{5,6},{6,7},{7,8},{8,9},{9,10},{10,1... | collective-permute-start | bytes 1572872 | tf_op jit(solution)/shard_map/while/body/eval_jaxpr/ppermute | solution.py:11
  210.4 10.8 %collective-permute-start = (bf16[2048,128]{1,0:T(8,128)(2,1)S(1)}, bf16[2048,128]{1,0:T(8,128)(2,1)S(1)}, u32[]{:S(2)}, u32[]{:S(2)}) collective-permute-start(bf16[2048,128]{1,0:T(8,128)(2,1)S(1)} %get-tuple-element.259), channel_id=1, source_target_pairs={{0,1},{1,2},{2,3},{3,4},{4,5},{5,6},{6,7},{7,8},{8,9},{9,10},{10,1... | collective-permute-start | bytes 1572872 | tf_op jit(solution)/shard_map/while/body/eval_jaxpr/ppermute | solution.py:11
  223.5 10.8 %collective-permute-start = (bf16[2048,128]{1,0:T(8,128)(2,1)S(1)}, bf16[2048,128]{1,0:T(8,128)(2,1)S(1)}, u32[]{:S(2)}, u32[]{:S(2)}) collective-permute-start(bf16[2048,128]{1,0:T(8,128)(2,1)S(1)} %get-tuple-element.259), channel_id=1, source_target_pairs={{0,1},{1,2},{2,3},{3,4},{4,5},{5,6},{6,7},{7,8},{8,9},{9,10},{10,1... | collective-permute-start | bytes 1572872 | tf_op jit(solution)/shard_map/while/body/eval_jaxpr/ppermute | solution.py:11
  236.6 10.8 %collective-permute-start = (bf16[2048,128]{1,0:T(8,128)(2,1)S(1)}, bf16[2048,128]{1,0:T(8,128)(2,1)S(1)}, u32[]{:S(2)}, u32[]{:S(2)}) collective-permute-start(bf16[2048,128]{1,0:T(8,128)(2,1)S(1)} %get-tuple-element.259), channel_id=1, source_target_pairs={{0,1},{1,2},{2,3},{3,4},{4,5},{5,6},{6,7},{7,8},{8,9},{9,10},{10,1... | collective-permute-start | bytes 1572872 | tf_op jit(solution)/shard_map/while/body/eval_jaxpr/ppermute | solution.py:11
  249.7 10.8 %collective-permute-start = (bf16[2048,128]{1,0:T(8,128)(2,1)S(1)}, bf16[2048,128]{1,0:T(8,128)(2,1)S(1)}, u32[]{:S(2)}, u32[]{:S(2)}) collective-permute-start(bf16[2048,128]{1,0:T(8,128)(2,1)S(1)} %get-tuple-element.259), channel_id=1, source_target_pairs={{0,1},{1,2},{2,3},{3,4},{4,5},{5,6},{6,7},{7,8},{8,9},{9,10},{10,1... | collective-permute-start | bytes 1572872 | tf_op jit(solution)/shard_map/while/body/eval_jaxpr/ppermute | solution.py:11
  262.8 10.8 %collective-permute-start = (bf16[2048,128]{1,0:T(8,128)(2,1)S(1)}, bf16[2048,128]{1,0:T(8,128)(2,1)S(1)}, u32[]{:S(2)}, u32[]{:S(2)}) collective-permute-start(bf16[2048,128]{1,0:T(8,128)(2,1)S(1)} %get-tuple-element.259), channel_id=1, source_target_pairs={{0,1},{1,2},{2,3},{3,4},{4,5},{5,6},{6,7},{7,8},{8,9},{9,10},{10,1... | collective-permute-start | bytes 1572872 | tf_op jit(solution)/shard_map/while/body/eval_jaxpr/ppermute | solution.py:11
  275.8 2.4 copy-start.4
  275.9 2.4 copy-start.11
  275.9 2.4 copy-start.13
  284.0 2.4 copy-start.9
  284.0 3.6 copy-start.8
  284.9 231.5 %reduce-scatter.5.cloned.1.call-start = ((), (), s32[]{:S(2)}) async-start(), calls=%async_computation.4 | async-start | bytes 4718592 | tf_op jit(solution)/shard_map/reduce_scatter | solution.py:106
  290.5 298.6 %reduce-scatter.3.cloned.1.call-start = ((), (), s32[]{:S(2)}) async-start(), calls=%async_computation.3 | async-start | bytes 8912896 | tf_op jit(solution)/shard_map/reduce_scatter | solution.py:95
  344.1 245.0 %copy-start.6 = (bf16[128,256]{1,0:T(8,128)(2,1)S(1)}, bf16[128,256]{1,0:T(8,128)(2,1)}, u32[]{:S(2)}) copy-start(bf16[128,256]{1,0:T(8,128)(2,1)} %param.22) | copy-start | bytes 196612
  431.0 160.7 %copy-start.1 = (bf16[128,256]{1,0:T(8,128)(2,1)S(1)}, bf16[128,256]{1,0:T(8,128)(2,1)}, u32[]{:S(2)}) copy-start(bf16[128,256]{1,0:T(8,128)(2,1)} %param.23) | copy-start | bytes 196612
Sparse Core Ops, SparseCore 0:
  10.4 74.4 all-gather.1
  285.0 145.9 all-reduce.2
  434.8 81.4 reduce-scatter.4
  518.6 70.4 reduce-scatter.2
where the time goes:
time: 603 us; the launch traced here: 598 us
  waiting for transfers between devices  350 us (58%)
  blocking collectives  71.1 us (12%)
  matrix products  63.8 us (11%)
  local copies, waits for them, and re-layouts  50.2 us (8%)
  other arithmetic  35.1 us (6%)
  between operations  14 us (2%)
  starting transfers between devices  13 us (2%)
    ppermute x15, waiting for transfers between devices, passed_along(): return lax.ppermute(x, axis, [(i, (i + by) % peers) for i in range(peers)])  130 us
    reduce_scatter x1, waiting for transfers between devices, shards(): lax.psum_scatter(placed.reshape(peer_count * row_count, in_width).astype(...  82.9 us
    reduce_scatter x1, waiting for transfers between devices, shards(): lax.psum_scatter(placed.reshape(slab_count * row_count, in_width).astype(...  72.7 us
    psum x1, blocking collectives, shards(): lax.psum((local_self, local_neigh, local_bias), ('wide', 'narrow'))  71.1 us
    all_gather x1, waiting for transfers between devices, shards(): lax.all_gather(features, 'wide', axis=0, tiled=True)  48.6 us
    dot_general x16, matrix products, band_add(): jnp.einsum('bij,bjf->bif', tiles_now, picked, preferred_element_type=jnp....  24.1 us
    dot_general x1, local copies, waits for them, and re-layouts, shards(): jnp.einsum('bsji,bjf->sbif', tile_half, signal, preferred_element_type=jn...  17.7 us
    psum x1, waiting for transfers between devices, shards(): lax.psum((local_self, local_neigh, local_bias), ('wide', 'narrow'))  15.2 us
  transfers between devices with their start and end apart: 19, of which 19 were waited for; matrix products, arithmetic and copies ran while one was open for 16% of the time, Pallas kernels for 0%

commit v1 on v0

v1 whole, which is shorter than its diff:
```python
import jax
import jax.numpy as jnp
from jax import lax
from jax.experimental import pallas as pl
from jax.experimental.pallas import tpu as pltpu
from jax.sharding import PartitionSpec as P

BF = jnp.bfloat16
F32 = jnp.float32
I32 = jnp.int32
MESH = pl.DeviceIdType.MESH
NT = (((1,), (1,)), ((), ()))
TN = (((0,), (0,)), ((), ()))

OFF = ((0, 0), (1, 0), (3, 0), (0, 1), (2, 0), (1, 1), (3, 1), (2, 1))
SEND = ((2, 1), (1, 1), (3, 1), (1, 0), (3, 0), (2, 0), (0, 1), (0, 0))
WIDE = 8
GELU_A = 0.7978845608
GELU_B = 0.044715

S_OWN, S_RELAY, S_PAIR, S_REQ, S_FET, S_PUSH = 0, 8, 16, 32, 40, 48
S_GPAIR, S_GW, S_GN, S_GA, S_GB, S_PART, S_RS, S_COUNT = 56, 57, 65, 73, 81, 82, 90, 104
L_TILE, L_FEAT, L_OFF, L_COT, L_IDX, L_LO, L_GF, L_G, L_COUNT = 0, 3, 4, 5, 6, 7, 8, 24, 25


def dot(a, b, dims=None):
    if dims is None:
        return jnp.dot(a, b, preferred_element_type=F32)
    return lax.dot_general(a, b, dims, preferred_element_type=F32)


def body(
    feat, tiles, cols, cols_v, offs, rblock, rrow, rvalid, w_self, w_neigh, bias, cot,
    lo_out, gf_out, g_out,
    f0, f1, f2, f3, f4, f5, f6, f7,
    tileb, stage, offi, offb, cotv, acc, degs, fa, gp, lo, sigt, runs, wcat,
    sd2d, rd2d, pbuf, rz, rxp, rxm, rha, rhb, rfp, rfm, rfz, baset, gfv,
    idx_v, idx, reqs, reqr, sel, fetr, pull, pushs, pushr,
    gsrc, grx, gsum, gwr, gown, gnr, gfin, gall,
    ss, rs, ls,
):
    fs = (f0, f1, f2, f3, f4, f5, f6, f7)
    me = lax.axis_index("narrow")
    w = lax.axis_index("wide")
    core = me % 2
    chip = me // 2
    x = chip % 4
    z = chip // 4

    def chip_at(dx, dz):
        return ((z + dz) % 2) * 4 + (x + dx) % 4

    def near(dx, dz):
        return (w, chip_at(dx, dz) * 2 + core)

    partner = (w, chip * 2 + (1 - core))
    xp, xm, zz = near(1, 0), near(3, 0), near(0, 1)

    def far(j):
        return ((w + j) % WIDE, me)

    pending = []

    def remote(src, dst, i, dev):
        return pltpu.make_async_remote_copy(
            src_ref=src, dst_ref=dst, send_sem=ss.at[i], recv_sem=rs.at[i],
            device_id=dev, device_id_type=MESH,
        )

    def send(src, dst, i, dev):
        c = remote(src, dst, i, dev)
        c.start()
        pending.append(c)
        return c

    def load_tiles(b, slot):
        return pltpu.make_async_copy(tiles.at[b], stage.at[slot], ls.at[L_TILE + slot])

    own = pltpu.make_async_copy(feat, f0.at[core], ls.at[L_FEAT])
    own.start()
    off_load = pltpu.make_async_copy(offs, offi, ls.at[L_OFF])
    off_load.start()
    load_tiles(0, 0).start()
    load_tiles(1, 1).start()
    cot_load = pltpu.make_async_copy(cot, cotv, ls.at[L_COT])
    cot_load.start()

    bar = pltpu.get_barrier_semaphore()
    pl.semaphore_signal(bar, inc=1, device_id=partner, device_id_type=MESH)
    for dx, dz in OFF[1:]:
        pl.semaphore_signal(bar, inc=1, device_id=near(dx, dz), device_id_type=MESH)
    for j in range(1, WIDE):
        pl.semaphore_signal(bar, inc=1, device_id=far(j), device_id_type=MESH)
    for b in range(WIDE):
        reqs[b] = jnp.full((8, 128), rblock[0, b], I32)
    pl.semaphore_wait(bar, 15)

    lo_h, hi_h = pl.ds(0, 8), pl.ds(8, 8)
    halves = (lo_h, hi_h)
    to_p = [None, None]
    to_m = [None, None]
    to_z = [None, None]
    to_p[0] = send(feat.at[lo_h], f2.at[core, lo_h], S_OWN + 0, xp)
    to_m[1] = send(feat.at[hi_h], f1.at[core, hi_h], S_OWN + 1, xm)
    to_z[0] = send(feat.at[lo_h], f3.at[core, lo_h], S_OWN + 2, zz)
    req_c = [None] * WIDE
    for j in range(1, WIDE):
        req_c[j] = send(reqs.at[(w + j) % WIDE], reqr.at[WIDE - j], S_REQ + j, far(j))
    to_p[1] = send(feat.at[hi_h], f2.at[core, hi_h], S_OWN + 3, xp)
    to_m[0] = send(feat.at[lo_h], f1.at[core, lo_h], S_OWN + 4, xm)
    to_z[1] = send(feat.at[hi_h], f3.at[core, hi_h], S_OWN + 5, zz)
    pair0 = send(feat, f0.at[core], S_PAIR, partner)

    c16 = cols_v[...]
    ib = lax.broadcasted_iota(I32, (16, 16), 0)
    rank = jnp.zeros((16, 16), I32)
    prev = jnp.zeros((16, 16), I32)
    count = jnp.zeros((16, 16), I32)
    upto = jnp.zeros((16, 16), I32)
    for b in range(16):
        row = jnp.broadcast_to(c16[b : b + 1, :], (16, 16))
        same = row == c16
        before = same & (ib > b)
        rank += jnp.where((row < c16) | before, 1, 0)
        prev += jnp.where(before, 1, 0)
        count += jnp.where(row == ib, 1, 0)
        upto += jnp.where(row <= ib, 1, 0)
    order = jnp.zeros((16, 16), I32)
    keep = jnp.zeros((16, 16), I32)
    for b in range(16):
        hit = jnp.broadcast_to(rank[b : b + 1, :], (16, 16)) == ib
        order += jnp.where(hit, b, 0)
        keep += jnp.where(hit & (jnp.broadcast_to(prev[b : b + 1, :], (16, 16)) > 0), 1, 0)
    idx_v[...] = jnp.zeros((64, 128), I32)
    idx_v[0:16, 0:16] = order
    idx_v[16:32, 0:16] = keep
    idx_v[32:48, 0:16] = jnp.maximum(upto - 1, 0)
    idx_v[48:64, 0:16] = jnp.where(count > 0, 1, 0)
    idx_load = pltpu.make_async_copy(idx_v, idx, ls.at[L_IDX])
    idx_load.start()
    wcat[0:128, :] = w_self[...]
    wcat[128:256, :] = w_neigh[...]

    own.wait()
    off_load.wait()
    reqr[0] = reqs[w]
    for j in range(WIDE):
        offb[j] = (offi[j] * rvalid[0, j]).astype(BF)
    fet_c = [None] * WIDE
    for j in range(1, WIDE):
        req_c[j].wait_recv()
    for j in range(1, WIDE):
        asked = reqr[WIDE - j][0:1, :]

        def pick(t, total, asked=asked):
            m = jnp.where(asked == t, 1.0, 0.0)
            return total + f0[core, t].astype(F32) * m

        sel[j] = lax.fori_loop(0, 16, pick, jnp.zeros((128, 128), F32)).astype(BF)
        fet_c[j] = send(sel.at[j], fetr.at[j], S_FET + j, far(WIDE - j))

    def convert(b, carry):
        slot = b % 3
        load_tiles(b, slot).wait()

        @pl.when(b + 2 < 16)
        def _():
            load_tiles(b + 2, (b + 2) % 3).start()

        total = jnp.zeros((128, 128), I32)
        for c in range(8):
            lft = stage[slot, 2 * c]
            rgt = stage[slot, 2 * c + 1]
            total += lft + rgt
            tileb[b, c] = jnp.concatenate([lft, rgt], axis=1).astype(F32).astype(BF)
        for j in range(WIDE):
            use = jnp.where(rrow[0, j] == b, rvalid[0, j], 0)
            total += offi[j] * use
        degs[b] = total.astype(F32).astype(BF)
        return carry

    lax.fori_loop(0, 16, convert, 0)

    def band(b, o):
        c = chip_at(*OFF[o])
        rhs = jnp.concatenate(
            [fs[o][0, cols[b, 2 * c]], fs[o][1, cols[b, 2 * c + 1]]], axis=0
        )
        return dot(tileb[b, c], rhs)

    def across(o, h):
        return send(fs[o].at[core, halves[h]], fs[o].at[core, halves[h]], S_PAIR + 2 * o + h, partner)

    swap = [[None, None] for _ in OFF]
    to_p[0].wait_recv()
    rel_p = send(f2.at[core, lo_h], f4.at[core, lo_h], S_RELAY + 0, xp)
    to_m[1].wait_recv()
    rel_m = send(f1.at[core, hi_h], f4.at[core, hi_h], S_RELAY + 1, xm)
    swap[2][0] = across(2, 0)
    swap[1][1] = across(1, 1)
    to_z[0].wait_recv()
    z_p = [None, None]
    z_m = [None, None]
    z_p[0] = send(f3.at[core, lo_h], f6.at[core, lo_h], S_RELAY + 2, xp)
    z_m[0] = send(f3.at[core, lo_h], f5.at[core, lo_h], S_RELAY + 3, xm)
    swap[3][0] = across(3, 0)

    pair0.wait_recv()

    def first(b, carry):
        acc[b] = band(b, 0)
        return carry

    lax.fori_loop(0, 16, first, 0, unroll=2)

    to_z[1].wait_recv()
    z_p[1] = send(f3.at[core, hi_h], f6.at[core, hi_h], S_RELAY + 4, xp)
    z_m[1] = send(f3.at[core, hi_h], f5.at[core, hi_h], S_RELAY + 5, xm)
    swap[3][1] = across(3, 1)
    to_p[1].wait_recv()
    swap[2][1] = across(2, 1)
    to_m[0].wait_recv()
    swap[1][0] = across(1, 0)

    for j in range(1, WIDE):
        fet_c[j].wait_recv()
    fetr[0] = f0[core, rblock[0, w]]
    for j in range(WIDE):
        pull[j] = dot(offb[(w + j) % WIDE], fetr[j])

    for o in (1, 2, 3):
        swap[o][0].wait_recv()
        swap[o][1].wait_recv()

    def second(b, carry):
        total = acc[b] + band(b, 1) + band(b, 2) + band(b, 3)
        for j in range(WIDE):
            use = jnp.where(rrow[0, (w + j) % WIDE] == b, 1, 0).astype(F32)
            total += pull[j] * use
        acc[b] = total
        return carry

    lax.fori_loop(0, 16, second, 0, unroll=2)

    rel_p.wait_recv()
    zr = [None, None]
    zr[0] = send(f4.at[core, lo_h], f7.at[core, lo_h], S_RELAY + 6, zz)
    swap[4][0] = across(4, 0)
    rel_m.wait_recv()
    zr[1] = send(f4.at[core, hi_h], f7.at[core, hi_h], S_RELAY + 7, zz)
    swap[4][1] = across(4, 1)
    swap[4][0].wait_recv()
    swap[4][1].wait_recv()

    def third(b, carry):
        acc[b] += band(b, 4)
        return carry

    lax.fori_loop(0, 16, third, 0, unroll=2)
    idx_load.wait()
    cot_load.wait()

    for h in range(2):
        z_p[h].wait_recv()
        swap[6][h] = across(6, h)
        z_m[h].wait_recv()
        swap[5][h] = across(5, h)
        zr[h].wait_recv()
        swap[7][h] = across(7, h)
    for o in (5, 6, 7):
        swap[o][0].wait_recv()
        swap[o][1].wait_recv()

    ones = jnp.ones((128, 128), BF)

    def dense(b, carry):
        total = acc[b] + band(b, 5) + band(b, 6) + band(b, 7)
        deg = degs[b]
        agg = (total / (dot(deg, ones) + 1.0)).astype(BF)
        both = jnp.concatenate([f0[core, b], agg], axis=1)
        fa[b] = both
        v = dot(both, wcat[...]) + bias[...].astype(F32)
        v2 = v * v
        th = jnp.tanh(GELU_A * (v + GELU_B * v * v2))
        up = 0.5 * (1.0 + th)
        lo[b] = (v * up).astype(BF)
        slope = up + 0.5 * v * (1.0 - th * th) * (GELU_A + (3.0 * GELU_A * GELU_B) * v2)
        g = (cotv[b].astype(F32) * slope).astype(BF)
        gp[b] = g
        back = dot(w_neigh[...], g, NT)
        sigt[b] = (back / (dot(ones, deg, NT) + 1.0)).astype(BF)
        return carry

    lax.fori_loop(0, 16, dense, 0, unroll=2)
    lo_c = pltpu.make_async_copy(lo, lo_out, ls.at[L_LO])
    lo_c.start()

    def product(n2, k):
        b = idx[k, n2]
        lanes = pl.ds(pl.multiple_of((n2 % 2) * 128, 128), 128)
        return dot(sigt[b], tileb[b, n2 // 2, :, lanes])

    def part(n2):
        total = product(n2, 0)
        runs[0] = total
        for k in range(1, 16):
            total = total * idx[16 + k, n2].astype(F32) + product(n2, k)
            runs[k] = total

    def run_of(n2, t):
        return runs[idx[32 + t, n2]] * idx[48 + t, n2].astype(F32)

    def chip_of(j):
        dx, dz = 0, 0
        for i, (ax, az) in enumerate(SEND):
            dx = dx + jnp.where(j == i, ax, 0)
            dz = dz + jnp.where(j == i, az, 0)
        return chip_at(dx, dz)

    def swap_part(j):
        return remote(sd2d.at[j], rd2d.at[j], S_PART + j, partner)

    def link(i, src, dst, dev):
        return remote(src, dst, S_RS + i, dev)

    leaf = [
        link(0, pbuf.at[0], rz, zz),
        link(1, pbuf.at[1], rxm, xp),
        link(2, pbuf.at[2], rxp, xm),
        link(3, pbuf.at[3, hi_h], rfm.at[hi_h], xp),
        link(4, pbuf.at[4, lo_h], rfp.at[lo_h], xm),
    ]

    def step(j, carry):
        @pl.when(j < 8)
        def _():
            n2 = chip_of(j) * 2 + (1 - core)
            part(n2)
            for t in range(16):
                sd2d[j, t] = run_of(n2, t).astype(BF)
            swap_part(j).start()

        @pl.when(j > 0)
        def _():
            i = j - 1
            n2 = chip_of(i) * 2 + core
            part(n2)
            swap_part(i).wait_recv()
            for t in range(16):
                pbuf[i, t] = (run_of(n2, t) + rd2d[i, t].astype(F32)).astype(BF)
            for q in range(5):

                @pl.when(i == q)
                def _(q=q):
                    leaf[q].start()

        return carry

    lax.fori_loop(0, 9, step, 0)
    pending.extend(leaf)

    push_c = [None] * WIDE
    for j in range(WIDE):
        there = (w + j) % WIDE
        sums = dot(sigt[rrow[0, there]], offb[there]).astype(BF)
        if j:
            pushs[j] = sums
            push_c[j] = send(pushs.at[j], pushr.at[WIDE - j], S_PUSH + j, far(j))
        else:
            pushr[0] = sums

    gsum_w = jnp.zeros((256, 256), F32)

    def weights(b, tot):
        return tot + dot(fa[b], gp[b], TN)

    def biases(b, tot):
        return tot + dot(jnp.ones((8, 128), BF), gp[b])

    grad_w = lax.fori_loop(0, 16, weights, gsum_w)
    grad_b = lax.fori_loop(0, 16, biases, jnp.zeros((8, 256), F32))
    for h in range(2):
        for p in range(8):
            gsrc[h, p, 0:16] = grad_w[h * 128 + p * 16 : h * 128 + p * 16 + 16]
            gsrc[h, p, 16:24] = grad_b
    g_pair = send(gsrc.at[1 - core], grx, S_GPAIR, partner)

    def base(b, carry):
        baset[b] = dot(w_self[...], gp[b], NT)
        return carry

    lax.fori_loop(0, 16, base, 0, unroll=2)

    g_pair.wait_recv()
    gsum[...] = gsrc[core] + grx[...]
    gw_c = [None] * WIDE
    for j in range(1, WIDE):
        gw_c[j] = send(gsum.at[(w + j) % WIDE], gwr.at[WIDE - j], S_GW + j, far(j))

    leaf[0].wait_recv()

    def add_one(t, carry):
        pbuf[5, t] = (pbuf[5, t].astype(F32) + rz[t].astype(F32)).astype(BF)
        return carry

    lax.fori_loop(0, 16, add_one, 0)
    half_a = send(pbuf.at[5, lo_h], rha, S_RS + 5, xp)
    half_b = send(pbuf.at[5, hi_h], rhb, S_RS + 6, xm)

    leaf[1].wait_recv()
    leaf[2].wait_recv()

    def add_two(t, carry):
        both = rxp[t].astype(F32) + rxm[t].astype(F32)
        pbuf[6, t] = (pbuf[6, t].astype(F32) + both).astype(BF)
        return carry

    lax.fori_loop(0, 16, add_two, 0)
    last_z = send(pbuf.at[6], rfz, S_RS + 7, zz)

    for j in range(1, WIDE):
        gw_c[j].wait_recv()
    tot = gsum[w]
    for j in range(1, WIDE):
        tot += gwr[j]
    gown[...] = tot
    gn_c = [None] * WIDE
    for o in range(1, 8):
        gn_c[o] = send(gown, gnr.at[chip], S_GN + o, near(*OFF[o]))

    for j in range(1, WIDE):
        push_c[j].wait_recv()

    def off_back(t, carry):
        total = baset[t] + pbuf[7, t].astype(F32)
        for j in range(WIDE):
            m = jnp.where(reqr[j][0:1, :] == t, 1.0, 0.0)
            total += pushr[j].astype(F32) * m
        baset[t] = total
        return carry

    lax.fori_loop(0, 16, off_back, 0)

    for o in range(1, 8):
        gn_c[o].wait_recv()
    gnr[chip] = gown[...]
    tot = gnr[0]
    for c in range(1, 8):
        tot += gnr[c]
    gfin[w] = tot
    ga_c = [None] * WIDE
    for j in range(1, WIDE):
        ga_c[j] = send(gfin.at[w], gfin.at[w], S_GA + j, far(j))

    half_a.wait_recv()

    def add_a(t, carry):
        pbuf[3, t] = (pbuf[3, t].astype(F32) + rha[t].astype(F32)).astype(BF)
        return carry

    lax.fori_loop(0, 8, add_a, 0)
    last_p = send(pbuf.at[3, lo_h], rfm.at[lo_h], S_RS + 8, xp)
    half_b.wait_recv()

    def add_b(t, carry):
        pbuf[4, 8 + t] = (pbuf[4, 8 + t].astype(F32) + rhb[t].astype(F32)).astype(BF)
        return carry

    lax.fori_loop(0, 8, add_b, 0)
    last_m = send(pbuf.at[4, hi_h], rfp.at[hi_h], S_RS + 9, xm)

    for j in range(1, WIDE):
        ga_c[j].wait_recv()
    gall[core] = gfin[...]
    g_last = send(gfin, gall.at[core], S_GB, partner)

    leaf[3].wait_recv()
    leaf[4].wait_recv()
    last_z.wait_recv()
    g_last.wait_recv()
    g_c = pltpu.make_async_copy(gall, g_out, ls.at[L_G])
    g_c.start()

    gf_c = []

    def finish(h):
        for i in range(8):
            t = 8 * h + i
            total = baset[t] + rfp[t].astype(F32) + rfm[t].astype(F32) + rfz[t].astype(F32)
            gfv[t] = total.T
            c = pltpu.make_async_copy(gfv.at[t], gf_out.at[t], ls.at[L_GF + t])
            c.start()
            gf_c.append(c)

    last_p.wait_recv()
    finish(0)
    last_m.wait_recv()
    finish(1)

    for c in gf_c:
        c.wait()
    lo_c.wait()
    g_c.wait()
    for c in pending:
        c.wait_send()

    def drain(j, carry):
        swap_part(j).wait_send()
        return carry

    lax.fori_loop(0, 8, drain, 0)


def shards(
    features, band_tiles, band_cols, off_tiles, req_block, req_row, req_valid,
    weight_self, weight_neigh, bias_term, cotangent,
):
    hbm = pl.BlockSpec(memory_space=pl.ANY)
    vmem = pl.BlockSpec(memory_space=pltpu.VMEM)
    smem = pl.BlockSpec(memory_space=pltpu.SMEM)
    block = (16, 128, 128)
    v = pltpu.VMEM
    scratch = [v((2,) + block, BF) for _ in range(8)]
    scratch += [
        v((16, 8, 128, 256), BF),
        v((3,) + block, I32),
        v((8, 128, 128), I32),
        v((8, 128, 128), BF),
        v((16, 128, 256), BF),
        v(block, F32),
        v(block, BF),
        v((16, 128, 256), BF),
        v((16, 128, 256), BF),
        v((16, 128, 256), BF),
        v(block, BF),
        v(block, F32),
        v((256, 256), BF),
        v((8,) + block, BF),
        v((8,) + block, BF),
        v((8,) + block, BF),
        v(block, BF),
        v(block, BF),
        v(block, BF),
        v((8, 128, 128), BF),
        v((8, 128, 128), BF),
        v(block, BF),
        v(block, BF),
        v(block, BF),
        v(block, F32),
        v(block, F32),
        v((64, 128), I32),
        pltpu.SMEM((64, 128), I32),
        v((8, 8, 128), I32),
        v((8, 8, 128), I32),
        v((8, 128, 128), BF),
        v((8, 128, 128), BF),
        v((8, 128, 128), F32),
        v((8, 128, 128), BF),
        v((8, 128, 128), BF),
        v((2, 8, 24, 256), F32),
        v((8, 24, 256), F32),
        v((8, 24, 256), F32),
        v((8, 24, 256), F32),
        v((24, 256), F32),
        v((8, 24, 256), F32),
        v((8, 24, 256), F32),
        v((2, 8, 24, 256), F32),
        pltpu.SemaphoreType.DMA((S_COUNT,)),
        pltpu.SemaphoreType.DMA((S_COUNT,)),
        pltpu.SemaphoreType.DMA((L_COUNT,)),
    ]
    layer_out, grad_feat, grads = pl.pallas_call(
        body,
        out_shape=(
            jax.ShapeDtypeStruct((16, 128, 256), BF),
            jax.ShapeDtypeStruct(block, F32),
            jax.ShapeDtypeStruct((2, 8, 24, 256), F32),
        ),
        in_specs=[hbm, hbm, smem, vmem, hbm, smem, smem, smem, vmem, vmem, vmem, hbm],
        out_specs=(hbm, hbm, hbm),
        scratch_shapes=scratch,
        compiler_params=pltpu.CompilerParams(
            collective_id=0, has_side_effects=True, vmem_limit_bytes=60 * 1024 * 1024
        ),
        name="sage",
    )(
        features.reshape(block), band_tiles, band_cols, band_cols, off_tiles[0],
        req_block, req_row, req_valid, weight_self, weight_neigh,
        bias_term.reshape(1, 256), cotangent.reshape(16, 128, 256),
    )
    factor = 262144 ** (-0.5)
    grad_self = grads[0, :, 0:16].reshape(128, 256) * factor
    grad_neigh = grads[1, :, 0:16].reshape(128, 256) * factor
    grad_bias = grads[0, 0, 16] * factor
    return (
        layer_out.reshape(2048, 256),
        grad_feat.reshape(2048, 128),
        grad_self,
        grad_neigh,
        grad_bias,
    )


def solution(mesh):
    placed = (
        P(("wide", "narrow"), None),
        P(("wide", "narrow"), None, None, None),
        P(("wide", "narrow"), None),
        P(("wide", "narrow"), None, None, None),
        P(("wide", "narrow"), None),
        P(("wide", "narrow"), None),
        P(("wide", "narrow"), None),
        P(),
        P(),
        P(),
        P(("wide", "narrow"), None),
    )
    return jax.shard_map(
        shards,
        mesh=mesh,
        in_specs=placed,
        out_specs=(P(("wide", "narrow"), None), P(("wide", "narrow"), None), P(), P(), P()),
        check_vma=False,
    )
```

time: 603 us -> 114 us (0.19)
  waiting for transfers between devices: 350 us -> 0 us
  Pallas kernels: 0 us -> 104 us
  blocking collectives: 71.1 us -> 0 us
  matrix products: 63.8 us -> 0 us
  local copies, waits for them, and re-layouts: 50.2 us -> 5.74 us
  other arithmetic: 35.1 us -> 2.95 us
  between operations: 14 us -> 0.64 us
  starting transfers between devices: 13 us -> 0 us
    reduce_scatter x2 -> x0, waiting for transfers between devices: 156 us -> none  [the longest x1 82.9 us: shards(): lax.psum_scatter(placed.reshape(peer_count * row_count, in_width).astype(...]
    ppermute x15 -> x0, waiting for transfers between devices: 130 us -> none  [passed_along(): return lax.ppermute(x, axis, [(i, (i + by) % peers) for i in range(peers)])]
    pallas_call x0 -> x1, Pallas kernels: none -> 104 us  [shards(): pl.pallas_call(body, out_shape=(jax.ShapeDtypeStruct((16, 128, 256), BF),...]
    psum x1 -> x0, blocking collectives: 71.1 us -> none  [shards(): lax.psum((local_self, local_neigh, local_bias), ('wide', 'narrow'))]
    dot_general x28 -> x0, matrix products: 63.8 us -> none  [the longest x16 24.1 us: band_add(): jnp.einsum('bij,bjf->bif', tiles_now, picked, preferred_element_type=jnp....]
    all_gather x1 -> x0, waiting for transfers between devices: 48.6 us -> none  [shards(): lax.all_gather(features, 'wide', axis=0, tiled=True)]
    dot_general x1 -> x0, local copies, waits for them, and re-layouts: 17.7 us -> none  [shards(): jnp.einsum('bsji,bjf->sbif', tile_half, signal, preferred_element_type=jn...]
    psum x1 -> x0, waiting for transfers between devices: 15.2 us -> none  [shards(): lax.psum((local_self, local_neigh, local_bias), ('wide', 'narrow'))]
  transfers between devices with their start and end apart: 19 -> 0, of which waited for: 19 -> 0; matrix products, arithmetic and copies ran while one was open for 16% -> 0% of each run, Pallas kernels for 0% -> 0%
where the time goes in v1:
time: 114 us
  Pallas kernels  104 us (91%)
  local copies, waits for them, and re-layouts  5.74 us (5%)
  other arithmetic  2.95 us (3%)
    pallas_call x1, Pallas kernels, shards(): pl.pallas_call(body, out_shape=(jax.ShapeDtypeStruct((16, 128, 256), BF),...  104 us
    unnamed x2, local copies, waits for them, and re-layouts  4.52 us

profile of v1, /device:TPU:1, one launch (start us, length us, event | category | flops | bytes accessed | tf_op | source)
XLA Modules:
  0.0 113.5 jit_solution(9692931890394555774)
XLA Ops:
  0.6 1.2 %reshape.32.bias = bf16[1,256]{1,0:T(2,128)(2,1)} reshape(bf16[256]{0:T(256)(128)(2,1)} %param.20) | data formatting | bytes 1024 | tf_op jit(solution)/shard_map/reshape | solution.py:589
  1.9 104.2 %sage.1 = (bf16[16,128,256]{2,1,0:T(8,128)(2,1)}, f32[16,128,128]{2,1,0:T(8,128)}, f32[2,8,24,256]{3,2,1,0:T(8,128)}) custom-call(bf16[16,128,128]{2,1,0:T(8,128)(2,1)} %bitcast.11, s32[16,16,128,128]{3,2,1,0:T(8,128)} %tiles.1, s32[16,16]{1,0:T(8,128)} %cols_v.1, s32[16,16]{1,0:T(8,128)} %cols_v.1, s32[8,128,128]{2,1,0:T(8,128)} %bitcast.12, ...), custom_call_target="tpu_custom_call" | custom-call | tf_op jit(solution)/shard_map/sage/pallas_call | solution.py:572
  106.1 1.7 %slice_multiply_fusion = (f32[1,8,16,256]{3,2,1,0:T(8,128)}, f32[1,8,16,256]{3,2,1,0:T(8,128)}) fusion(f32[2,8,24,256]{3,2,1,0:T(8,128)} %get-tuple-element.10), kind=kLoop, calls=%fused_computation | loop fusion | flops 65536 | bytes 524288 | tf_op jit(solution)/shard_map/mul | solution.py:593
  107.8 1.3 %slice_multiply_fusion.2 = f32[1,1,1,256]{3,2,1,0:T(1,128)} fusion(f32[2,8,24,256]{3,2,1,0:T(8,128)} %get-tuple-element.10), kind=kLoop, calls=%fused_computation.2 | loop fusion | flops 256 | bytes 2048 | tf_op jit(solution)/shard_map/mul | solution.py:594
  109.0 2.3 %copy.18 = bf16[2048,256]{1,0:T(8,128)(2,1)} copy(bf16[2048,256]{1,0:T(8,128)(2,1)} %bitcast.10) | data formatting | bytes 2097152
  111.3 2.3 %copy.19 = f32[2048,128]{1,0:T(8,128)} copy(f32[2048,128]{1,0:T(8,128)} %bitcast.9) | data formatting | bytes 2097152

commit v2 on v1

--- a/solution.py
+++ b/solution.py
@@ -100,12 +100,12 @@
     to_p = [None, None]
     to_m = [None, None]
     to_z = [None, None]
+    req_c = [None] * WIDE
+    for j in range(1, WIDE):
+        req_c[j] = send(reqs.at[(w + j) % WIDE], reqr.at[WIDE - j], S_REQ + j, far(j))
     to_p[0] = send(feat.at[lo_h], f2.at[core, lo_h], S_OWN + 0, xp)
     to_m[1] = send(feat.at[hi_h], f1.at[core, hi_h], S_OWN + 1, xm)
     to_z[0] = send(feat.at[lo_h], f3.at[core, lo_h], S_OWN + 2, zz)
-    req_c = [None] * WIDE
-    for j in range(1, WIDE):
-        req_c[j] = send(reqs.at[(w + j) % WIDE], reqr.at[WIDE - j], S_REQ + j, far(j))
     to_p[1] = send(feat.at[hi_h], f2.at[core, hi_h], S_OWN + 3, xp)
     to_m[0] = send(feat.at[lo_h], f1.at[core, lo_h], S_OWN + 4, xm)
     to_z[1] = send(feat.at[hi_h], f3.at[core, hi_h], S_OWN + 5, zz)
@@ -143,21 +143,6 @@
 
     own.wait()
     off_load.wait()
-    reqr[0] = reqs[w]
-    for j in range(WIDE):
-        offb[j] = (offi[j] * rvalid[0, j]).astype(BF)
-    fet_c = [None] * WIDE
-    for j in range(1, WIDE):
-        req_c[j].wait_recv()
-    for j in range(1, WIDE):
-        asked = reqr[WIDE - j][0:1, :]
-
-        def pick(t, total, asked=asked):
-            m = jnp.where(asked == t, 1.0, 0.0)
-            return total + f0[core, t].astype(F32) * m
-
-        sel[j] = lax.fori_loop(0, 16, pick, jnp.zeros((128, 128), F32)).astype(BF)
-        fet_c[j] = send(sel.at[j], fetr.at[j], S_FET + j, far(WIDE - j))
 
     def convert(b, carry):
         slot = b % 3
@@ -179,7 +164,23 @@
         degs[b] = total.astype(F32).astype(BF)
         return carry
 
-    lax.fori_loop(0, 16, convert, 0)
+    lax.fori_loop(0, 6, convert, 0)
+
+    reqr[0] = reqs[w]
+    for j in range(WIDE):
+        offb[j] = (offi[j] * rvalid[0, j]).astype(BF)
+    fet_c = [None] * WIDE
+    for j in range(1, WIDE):
+        req_c[j].wait_recv()
+    for j in range(1, WIDE):
+        asked = reqr[WIDE - j][0:1, :]
+
+        def pick(t, total, asked=asked):
+            m = jnp.where(asked == t, 1.0, 0.0)
+            return total + f0[core, t].astype(F32) * m
+
+        sel[j] = lax.fori_loop(0, 16, pick, jnp.zeros((128, 128), F32)).astype(BF)
+        fet_c[j] = send(sel.at[j], fetr.at[j], S_FET + j, far(WIDE - j))
 
     def band(b, o):
         c = chip_at(*OFF[o])
@@ -205,6 +206,7 @@
     z_m[0] = send(f3.at[core, lo_h], f5.at[core, lo_h], S_RELAY + 3, xm)
     swap[3][0] = across(3, 0)
 
+    lax.fori_loop(6, 16, convert, 0)
     pair0.wait_recv()
 
     def first(b, carry):
@@ -222,21 +224,12 @@
     to_m[0].wait_recv()
     swap[1][0] = across(1, 0)
 
-    for j in range(1, WIDE):
-        fet_c[j].wait_recv()
-    fetr[0] = f0[core, rblock[0, w]]
-    for j in range(WIDE):
-        pull[j] = dot(offb[(w + j) % WIDE], fetr[j])
-
     for o in (1, 2, 3):
         swap[o][0].wait_recv()
         swap[o][1].wait_recv()
 
     def second(b, carry):
         total = acc[b] + band(b, 1) + band(b, 2) + band(b, 3)
-        for j in range(WIDE):
-            use = jnp.where(rrow[0, (w + j) % WIDE] == b, 1, 0).astype(F32)
-            total += pull[j] * use
         acc[b] = total
         return carry
 
@@ -249,11 +242,21 @@
     rel_m.wait_recv()
     zr[1] = send(f4.at[core, hi_h], f7.at[core, hi_h], S_RELAY + 7, zz)
     swap[4][1] = across(4, 1)
+    for j in range(1, WIDE):
+        fet_c[j].wait_recv()
+    fetr[0] = f0[core, rblock[0, w]]
+    for j in range(WIDE):
+        pull[j] = dot(offb[(w + j) % WIDE], fetr[j])
+
     swap[4][0].wait_recv()
     swap[4][1].wait_recv()
 
     def third(b, carry):
-        acc[b] += band(b, 4)
+        total = acc[b] + band(b, 4)
+        for j in range(WIDE):
+            use = jnp.where(rrow[0, (w + j) % WIDE] == b, 1, 0).astype(F32)
+            total += pull[j] * use
+        acc[b] = total
         return carry
 
     lax.fori_loop(0, 16, third, 0, unroll=2)
@@ -279,7 +282,7 @@
         agg = (total / (dot(deg, ones) + 1.0)).astype(BF)
         both = jnp.concatenate([f0[core, b], agg], axis=1)
         fa[b] = both
-        v = dot(both, wcat[...]) + bias[...].astype(F32)
+        v = dot(both, wcat[...]) + bias[...].astype(F32).reshape(1, 256)
         v2 = v * v
         th = jnp.tanh(GELU_A * (v + GELU_B * v * v2))
         up = 0.5 * (1.0 + th)
@@ -348,7 +351,7 @@
             swap_part(i).wait_recv()
             for t in range(16):
                 pbuf[i, t] = (run_of(n2, t) + rd2d[i, t].astype(F32)).astype(BF)
-            for q in range(5):
+            for q in range(3):
 
                 @pl.when(i == q)
                 def _(q=q):
@@ -407,17 +410,6 @@
     half_a = send(pbuf.at[5, lo_h], rha, S_RS + 5, xp)
     half_b = send(pbuf.at[5, hi_h], rhb, S_RS + 6, xm)
 
-    leaf[1].wait_recv()
-    leaf[2].wait_recv()
-
-    def add_two(t, carry):
-        both = rxp[t].astype(F32) + rxm[t].astype(F32)
-        pbuf[6, t] = (pbuf[6, t].astype(F32) + both).astype(BF)
-        return carry
-
-    lax.fori_loop(0, 16, add_two, 0)
-    last_z = send(pbuf.at[6], rfz, S_RS + 7, zz)
-
     for j in range(1, WIDE):
         gw_c[j].wait_recv()
     tot = gsum[w]
@@ -427,6 +419,20 @@
     gn_c = [None] * WIDE
     for o in range(1, 8):
         gn_c[o] = send(gown, gnr.at[chip], S_GN + o, near(*OFF[o]))
+
+    leaf[3].start()
+    leaf[4].start()
+
+    leaf[1].wait_recv()
+    leaf[2].wait_recv()
+
+    def add_two(t, carry):
+        both = rxp[t].astype(F32) + rxm[t].astype(F32)
+        pbuf[6, t] = (pbuf[6, t].astype(F32) + both).astype(BF)
+        return carry
+
+    lax.fori_loop(0, 16, add_two, 0)
+    last_z = send(pbuf.at[6], rfz, S_RS + 7, zz)
 
     for j in range(1, WIDE):
         push_c[j].wait_recv()
@@ -440,6 +446,23 @@
         return carry
 
     lax.fori_loop(0, 16, off_back, 0)
+
+    half_a.wait_recv()
+
+    def add_a(t, carry):
+        pbuf[3, t] = (pbuf[3, t].astype(F32) + rha[t].astype(F32)).astype(BF)
+        return carry
+
+    lax.fori_loop(0, 8, add_a, 0)
+    last_p = send(pbuf.at[3, lo_h], rfm.at[lo_h], S_RS + 8, xp)
+    half_b.wait_recv()
+
+    def add_b(t, carry):
+        pbuf[4, 8 + t] = (pbuf[4, 8 + t].astype(F32) + rhb[t].astype(F32)).astype(BF)
+        return carry
+
+    lax.fori_loop(0, 8, add_b, 0)
+    last_m = send(pbuf.at[4, hi_h], rfp.at[hi_h], S_RS + 9, xm)
 
     for o in range(1, 8):
         gn_c[o].wait_recv()
@@ -452,23 +475,6 @@
     for j in range(1, WIDE):
         ga_c[j] = send(gfin.at[w], gfin.at[w], S_GA + j, far(j))
 
-    half_a.wait_recv()
-
-    def add_a(t, carry):
-        pbuf[3, t] = (pbuf[3, t].astype(F32) + rha[t].astype(F32)).astype(BF)
-        return carry
-
-    lax.fori_loop(0, 8, add_a, 0)
-    last_p = send(pbuf.at[3, lo_h], rfm.at[lo_h], S_RS + 8, xp)
-    half_b.wait_recv()
-
-    def add_b(t, carry):
-        pbuf[4, 8 + t] = (pbuf[4, 8 + t].astype(F32) + rhb[t].astype(F32)).astype(BF)
-        return carry
-
-    lax.fori_loop(0, 8, add_b, 0)
-    last_m = send(pbuf.at[4, hi_h], rfp.at[hi_h], S_RS + 9, xm)
-
     for j in range(1, WIDE):
         ga_c[j].wait_recv()
     gall[core] = gfin[...]
@@ -509,6 +515,34 @@
         return carry
 
     lax.fori_loop(0, 8, drain, 0)
+
+
+def settle(lo_in, gf_in, g_in, lo_out, gf_out, gs_out, gn_out, gb_out, lov, gfv, gv, ls):
+    count = 4
+    g_c = pltpu.make_async_copy(g_in, gv, ls.at[4 * count])
+    g_c.start()
+    loads = []
+    stores = []
+    for i in range(count):
+        part = pl.ds(4 * i, 4)
+        for k, (src, mid, dst) in enumerate(((lo_in, lov, lo_out), (gf_in, gfv, gf_out))):
+            n = 2 * i + k
+            loads.append(pltpu.make_async_copy(src.at[part], mid.at[part], ls.at[n]))
+            stores.append(
+                pltpu.make_async_copy(mid.at[part], dst.at[part], ls.at[2 * count + n])
+            )
+            loads[-1].start()
+    for load, store in zip(loads, stores):
+        load.wait()
+        store.start()
+    g_c.wait()
+    factor = 262144 ** (-0.5)
+    for p in range(8):
+        gs_out[p * 16 : p * 16 + 16] = gv[0, p, 0:16] * factor
+        gn_out[p * 16 : p * 16 + 16] = gv[1, p, 0:16] * factor
+    gb_out[...] = gv[0, 0, 16:17] * factor
+    for store in stores:
+        store.wait()
 
 
 def shards(
@@ -586,18 +620,33 @@
     )(
         features.reshape(block), band_tiles, band_cols, band_cols, off_tiles[0],
         req_block, req_row, req_valid, weight_self, weight_neigh,
-        bias_term.reshape(1, 256), cotangent.reshape(16, 128, 256),
+        bias_term, cotangent.reshape(16, 128, 256),
     )
-    factor = 262144 ** (-0.5)
-    grad_self = grads[0, :, 0:16].reshape(128, 256) * factor
-    grad_neigh = grads[1, :, 0:16].reshape(128, 256) * factor
-    grad_bias = grads[0, 0, 16] * factor
+    layer_out, grad_feat, grad_self, grad_neigh, grad_bias = pl.pallas_call(
+        settle,
+        out_shape=(
+            jax.ShapeDtypeStruct((16, 128, 256), BF),
+            jax.ShapeDtypeStruct(block, F32),
+            jax.ShapeDtypeStruct((128, 256), F32),
+            jax.ShapeDtypeStruct((128, 256), F32),
+            jax.ShapeDtypeStruct((1, 256), F32),
+        ),
+        in_specs=[hbm, hbm, hbm],
+        out_specs=(hbm, hbm, vmem, vmem, vmem),
+        scratch_shapes=[
+            v((16, 128, 256), BF),
+            v(block, F32),
+            v((2, 8, 24, 256), F32),
+            pltpu.SemaphoreType.DMA((17,)),
+        ],
+        name="settle",
+    )(layer_out, grad_feat, grads)
     return (
         layer_out.reshape(2048, 256),
         grad_feat.reshape(2048, 128),
         grad_self,
         grad_neigh,
-        grad_bias,
+        grad_bias.reshape(256),
     )
 
 

time: 114 us -> 102 us (0.89)
  local copies, waits for them, and re-layouts: 5.74 us -> 0 us
  Pallas kernels: 104 us -> 101 us
  other arithmetic: 2.95 us -> 0 us
    pallas_call x1, Pallas kernels: 104 us -> 98.1 us  [shards(): pl.pallas_call(body, out_shape=(jax.ShapeDtypeStruct((16, 128, 256), BF),...]
    unnamed x2 -> x0, local copies, waits for them, and re-layouts: 4.52 us -> none
    pallas_call x0 -> x1, Pallas kernels: none -> 3.22 us  [shards(): pl.pallas_call(settle, out_shape=(jax.ShapeDtypeStruct((16, 128, 256), BF...]
    mul x2 -> x0, other arithmetic: 2.95 us -> none  [the longest x1 1.69 us: shards(): grad_neigh = grads[1, :, 0:16].reshape(128, 256) * factor]
    reshape x1 -> x0, local copies, waits for them, and re-layouts: 1.22 us -> none  [shards(): bias_term.reshape(1, 256)]
where the time goes in v2:
time: 102 us
  Pallas kernels  101 us (99%)
    pallas_call x1, Pallas kernels, shards(): pl.pallas_call(body, out_shape=(jax.ShapeDtypeStruct((16, 128, 256), BF),...  98.1 us
    pallas_call x1, Pallas kernels, shards(): pl.pallas_call(settle, out_shape=(jax.ShapeDtypeStruct((16, 128, 256), BF...  3.22 us

profile of v2, /device:TPU:1, one launch (start us, length us, event | category | flops | bytes accessed | tf_op | source)
XLA Modules:
  0.0 102.0 jit_solution(16692109015930340321)
XLA Ops:
  0.6 98.1 %sage.1 = (bf16[16,128,256]{2,1,0:T(8,128)(2,1)}, f32[16,128,128]{2,1,0:T(8,128)}, f32[2,8,24,256]{3,2,1,0:T(8,128)}) custom-call(bf16[16,128,128]{2,1,0:T(8,128)(2,1)} %bitcast.7, s32[16,16,128,128]{3,2,1,0:T(8,128)} %tiles.1, s32[16,16]{1,0:T(8,128)} %cols_v.1, s32[16,16]{1,0:T(8,128)} %cols_v.1, s32[8,128,128]{2,1,0:T(8,128)} %bitcast.8, s32[1,8]{1,0:T(1,128)} %rblock.1, ...), custom_call_target="tpu_custom_call" | custom-call | tf_op jit(solution)/shard_map/sage/pallas_call | solution.py:606
  98.7 3.2 %settle.1 = (bf16[16,128,256]{2,1,0:T(8,128)(2,1)}, f32[16,128,128]{2,1,0:T(8,128)}, f32[128,256]{1,0:T(8,128)}, f32[128,256]{1,0:T(8,128)}, f32[1,256]{1,0:T(1,128)}) custom-call(bf16[16,128,256]{2,1,0:T(8,128)(2,1)} %get-tuple-element.13.lo_in, f32[16,128,128]{2,1,0:T(8,128)} %get-tuple-element.14.gf_in, f32[2,8,24,256]{3,2,1,0:T(8,128)} %get-tuple-element.15.g_in), custom_call_target="tpu_custom_call" | custom-call | tf_op jit(solution)/shard_map/settle/pallas_call | solution.py:625

commit v3 on v2

--- a/solution.py
+++ b/solution.py
@@ -20,7 +20,7 @@
 
 S_OWN, S_RELAY, S_PAIR, S_REQ, S_FET, S_PUSH = 0, 8, 16, 32, 40, 48
 S_GPAIR, S_GW, S_GN, S_GA, S_GB, S_PART, S_RS, S_COUNT = 56, 57, 65, 73, 81, 82, 90, 104
-L_TILE, L_FEAT, L_OFF, L_COT, L_IDX, L_LO, L_GF, L_G, L_COUNT = 0, 3, 4, 5, 6, 7, 8, 24, 25
+L_TILE, L_FEAT, L_OFF, L_COT, L_IDX, L_LO, L_GF, L_G, L_REQ, L_COUNT = 0, 3, 4, 5, 6, 7, 8, 24, 25, 26
 
 
 def dot(a, b, dims=None):
@@ -35,7 +35,7 @@
     f0, f1, f2, f3, f4, f5, f6, f7,
     tileb, stage, offi, offb, cotv, acc, degs, fa, gp, lo, sigt, runs, wcat,
     sd2d, rd2d, pbuf, rz, rxp, rxm, rha, rhb, rfp, rfm, rfz, baset, gfv,
-    idx_v, idx, reqs, reqr, sel, fetr, pull, pushs, pushr,
+    idx_v, idx, reqs, reqr, asked, sel, fetr, pull, pushs, pushr,
     gsrc, grx, gsum, gwr, gown, gnr, gfin, gall,
     ss, rs, ls,
 ):
@@ -172,14 +172,12 @@
     fet_c = [None] * WIDE
     for j in range(1, WIDE):
         req_c[j].wait_recv()
-    for j in range(1, WIDE):
-        asked = reqr[WIDE - j][0:1, :]
-
-        def pick(t, total, asked=asked):
-            m = jnp.where(asked == t, 1.0, 0.0)
-            return total + f0[core, t].astype(F32) * m
-
-        sel[j] = lax.fori_loop(0, 16, pick, jnp.zeros((128, 128), F32)).astype(BF)
+    ask_load = pltpu.make_async_copy(reqr, asked, ls.at[L_REQ])
+    ask_load.start()
+    pair0.wait_recv()
+    ask_load.wait()
+    for j in range(1, WIDE):
+        sel[j] = f0[core, asked[WIDE - j, 0, 0]]
         fet_c[j] = send(sel.at[j], fetr.at[j], S_FET + j, far(WIDE - j))
 
     def band(b, o):
@@ -207,7 +205,6 @@
     swap[3][0] = across(3, 0)
 
     lax.fori_loop(6, 16, convert, 0)
-    pair0.wait_recv()
 
     def first(b, carry):
         acc[b] = band(b, 0)
@@ -586,6 +583,7 @@
         pltpu.SMEM((64, 128), I32),
         v((8, 8, 128), I32),
         v((8, 8, 128), I32),
+        pltpu.SMEM((8, 8, 128), I32),
         v((8, 128, 128), BF),
         v((8, 128, 128), BF),
         v((8, 128, 128), F32),

time: 102 us -> 102 us (level)
  no operation moved by 1% of the time
where the time goes in v3:
time: 102 us
  Pallas kernels  101 us (99%)
    pallas_call x1, Pallas kernels, shards(): pl.pallas_call(body, out_shape=(jax.ShapeDtypeStruct((16, 128, 256), BF),...  98.1 us
    pallas_call x1, Pallas kernels, shards(): pl.pallas_call(settle, out_shape=(jax.ShapeDtypeStruct((16, 128, 256), BF...  3.22 us

profile of v3, /device:TPU:1, one launch (start us, length us, event | category | flops | bytes accessed | tf_op | source)
XLA Modules:
  0.0 102.0 jit_solution(9905080003288123849)
XLA Ops:
  0.6 98.1 %sage.1 = (bf16[16,128,256]{2,1,0:T(8,128)(2,1)}, f32[16,128,128]{2,1,0:T(8,128)}, f32[2,8,24,256]{3,2,1,0:T(8,128)}) custom-call(bf16[16,128,128]{2,1,0:T(8,128)(2,1)} %bitcast.7, s32[16,16,128,128]{3,2,1,0:T(8,128)} %tiles.1, s32[16,16]{1,0:T(8,128)} %cols_v.1, s32[16,16]{1,0:T(8,128)} %cols_v.1, s32[8,128,128]{2,1,0:T(8,128)} %bitcast.8, s32[1,8]{1,0:T(1,128)} %rblock.1, ...), custom_call_target="tpu_custom_call" | custom-call | tf_op jit(solution)/shard_map/sage/pallas_call | solution.py:604
  98.7 3.2 %settle.1 = (bf16[16,128,256]{2,1,0:T(8,128)(2,1)}, f32[16,128,128]{2,1,0:T(8,128)}, f32[128,256]{1,0:T(8,128)}, f32[128,256]{1,0:T(8,128)}, f32[1,256]{1,0:T(1,128)}) custom-call(bf16[16,128,256]{2,1,0:T(8,128)(2,1)} %get-tuple-element.13.lo_in, f32[16,128,128]{2,1,0:T(8,128)} %get-tuple-element.14.gf_in, f32[2,8,24,256]{3,2,1,0:T(8,128)} %get-tuple-element.15.g_in), custom_call_target="tpu_custom_call" | custom-call | tf_op jit(solution)/shard_map/settle/pallas_call | solution.py:623
